TPU v7x, 32 devices: a whole 2x2x4 slice. The times are simulated.
32 devices in a mesh: row: 8 (over z, x), col: 4 (over y, core).
Axes of the slice: x: 2, y: 2, z: 4, core: 2. Of those that a mesh axis runs over, the one named last changes fastest.
Arguments:
- mel: float32 [128, 18432], P('col', 'row'), may hold values from -6 to 6
- pair_val: int32 [128], replicated, may hold values from 0 to 31
- pair_cond: int32 [128], replicated, may hold values from 0 to 31
- val_energy: float32 [32], replicated, may hold values from -8 to -1
- cond_energy: float32 [32], replicated, may hold values from 1 to 8
- freqs: float32 [2], replicated, may hold values from 0.5 to 6
Outputs:
- chi: float32 [2, 18432, 18432], P(None, 'row', 'col')
All inputs are finite; a program needn't handle non-finite values.
Results may differ from a plain program's by a relative error of at most 0.000098.
Values sent between devices are 32-bit elements; how exact they have to be, the bound alone decides.
A program may use at most 128 MiB of HBM per device.

v0:
```python
import math
import jax
import jax.numpy as jnp
from jax import lax
from jax.sharding import PartitionSpec as P

PAIRS = 128


def body(mel, pair_val, pair_cond, val_energy, cond_energy, freqs):
    rows_all = lax.all_gather(mel, "col", axis=0, tiled=True)
    own_block = lax.all_gather(mel, "row", axis=1, tiled=True)
    col_block = lax.all_to_all(own_block, "col", split_axis=1, concat_axis=0, tiled=True)
    cond_onehot = (
        pair_cond[:, None] == jnp.arange(cond_energy.shape[0], dtype=jnp.int32)[None, :]
    ).astype(jnp.float32)
    val_onehot = (
        pair_val[:, None] == jnp.arange(val_energy.shape[0], dtype=jnp.int32)[None, :]
    ).astype(jnp.float32)
    gap = jnp.sum(cond_onehot * cond_energy[None, :], axis=1) - jnp.sum(
        val_onehot * val_energy[None, :], axis=1
    )
    scale = 1.0 / math.sqrt(PAIRS)
    weights = (
        -4.0
        * gap[None, :]
        / (gap[None, :] * gap[None, :] + freqs[:, None] * freqs[:, None])
        * scale
    )
    scaled = weights[:, :, None] * rows_all[None, :, :]
    return lax.dot_general(
        scaled,
        col_block,
        (((1,), (0,)), ((), ())),
        precision=lax.Precision.HIGHEST,
        preferred_element_type=jnp.float32,
    )


def solution(mesh):
    return jax.shard_map(
        body,
        mesh=mesh,
        in_specs=(P("col", "row"), P(), P(), P(), P(), P()),
        out_specs=P(None, "row", "col"),
        check_vma=False,
    )
```

profile of v0, /device:TPU:0, one launch (start us, length us, event | category | flops | bytes accessed | tf_op | source)
XLA Modules:
  0.0 184.6 jit_solution(5742177264491357623)
XLA Ops:
  6.5 0.0 all-gather.5.cloned.1.call-start
  6.5 0.7 all-gather.5.cloned.1.call-update
  7.3 0.0 all-gather.3.cloned.1.call-start
  7.3 0.7 all-gather.3.cloned.1.call-update
  8.0 56.1 %all-gather.5.cloned.1.call-done = f32[32,18432]{1,0:T(8,128)} async-done(((f32[32,2304]{1,0:T(8,128)}), f32[32,18432]{1,0:T(8,128)}) %all-gather.5.cloned.1.call-update) | async-done | bytes 2359312 | tf_op jit(solution)/shard_map/all_gather | solution.py:12
  64.1 3.2 %copy.13 = f32[4,4,8,4608]{3,2,0,1:T(8,128)} copy(f32[4,4,8,4608]{3,2,1,0:T(8,128)} %bitcast.13) | data formatting | bytes 4718592 | tf_op jit(solution)/shard_map/all_to_all | solution.py:13
  67.3 0.0 copy-start.4
  67.3 0.0 copy-start
  67.3 0.0 copy-start.1
  67.3 0.0 copy-start.2
  67.3 0.0 copy-start.3
  67.4 3.8 %all-to-all-start = ((f32[32,4,4608]{2,0,1:T(8,128)}), f32[32,4,4608]{2,0,1:T(8,128)S(1)}, u32[]{:S(2)}, u32[]{:S(2)}) async-start(f32[32,4,4608]{2,0,1:T(8,128)} %bitcast.12), calls=%async_computation | async-start | bytes 4718592 | tf_op jit(solution)/shard_map/all_to_all | solution.py:13
  71.2 0.0 copy-done.4
  71.2 0.0 copy-done
  71.2 0.0 copy-done.1
  71.2 0.0 copy-done.2
  71.2 0.0 copy-done.3
  71.2 0.1 select_reduce_fusion
  71.3 0.1 divide_multiply_fusion
  71.4 16.4 %all-gather.3.cloned.1.call-done = f32[128,2304]{1,0:T(8,128)} async-done(((f32[32,2304]{1,0:T(8,128)}), f32[128,2304]{1,0:T(8,128)}) %all-gather.3.cloned.1.call-update) | async-done | bytes 1179664 | tf_op jit(solution)/shard_map/all_gather | solution.py:11
  87.8 1.6 copy.9
  89.4 16.0 %all-to-all-done = f32[32,4,4608]{2,0,1:T(8,128)S(1)} async-done(((f32[32,4,4608]{2,0,1:T(8,128)}), f32[32,4,4608]{2,0,1:T(8,128)S(1)}, u32[]{:S(2)}, u32[]{:S(2)}) %all-to-all-start) | async-done | bytes 2359328 | tf_op jit(solution)/shard_map/all_to_all | solution.py:13
  105.4 72.3 %fusion = f32[2,2304,4608]{2,1,0:T(8,128)} fusion(f32[128,4608,1]{1,0,2:T(8,128)S(1)} %bitcast.11, f32[128,2304]{0,1:T(8,128)S(1)} %copy.9, f32[2,128]{1,0:T(2,128)S(1)} %divide_multiply_fusion), kind=kOutput, calls=%fused_computation.1 | convolution fusion | flops 32615497728 | bytes 88474624 | tf_op jit(solution)/shard_map/dot_general | solution.py:31
  (2 shorter events, 0.0 us)
Async XLA Ops:
  6.5 57.6 %all-gather.5.cloned.1.call-start = ((), (), s32[]{:S(2)}) async-start(), calls=%async_computation.2 | async-start | bytes 2654208 | tf_op jit(solution)/shard_map/all_gather | solution.py:12
  7.3 80.5 %all-gather.3.cloned.1.call-start = ((), (), s32[]{:S(2)}) async-start(), calls=%async_computation.1 | async-start | bytes 1474560 | tf_op jit(solution)/shard_map/all_gather | solution.py:11
  67.3 3.8 %copy-start.4 = (f32[2]{0:T(128)S(1)}, f32[2]{0:T(128)}, u32[]{:S(2)}) copy-start(f32[2]{0:T(128)} %param.11) | copy-start | bytes 28
  67.3 3.8 %copy-start = (f32[32]{0:T(128)S(1)}, f32[32]{0:T(128)}, u32[]{:S(2)}) copy-start(f32[32]{0:T(128)} %param.9) | copy-start | bytes 388
  67.3 3.9 %copy-start.1 = (s32[128]{0:T(128)S(1)}, s32[128]{0:T(128)}, u32[]{:S(2)}) copy-start(s32[128]{0:T(128)} %param.7) | copy-start | bytes 1540
  67.3 3.9 %copy-start.2 = (f32[32]{0:T(128)S(1)}, f32[32]{0:T(128)}, u32[]{:S(2)}) copy-start(f32[32]{0:T(128)} %param.10) | copy-start | bytes 388
  67.3 3.9 %copy-start.3 = (s32[128]{0:T(128)S(1)}, s32[128]{0:T(128)}, u32[]{:S(2)}) copy-start(s32[128]{0:T(128)} %param.8) | copy-start | bytes 1540
  67.4 38.1 %all-to-all-start = ((f32[32,4,4608]{2,0,1:T(8,128)}), f32[32,4,4608]{2,0,1:T(8,128)S(1)}, u32[]{:S(2)}, u32[]{:S(2)}) async-start(f32[32,4,4608]{2,0,1:T(8,128)} %bitcast.12), calls=%async_computation | async-start | bytes 4718592 | tf_op jit(solution)/shard_map/all_to_all | solution.py:13
Sparse Core Ops, SparseCore 0:
  9.5 54.5 all-gather.4
  65.7 22.0 all-gather.2
where the time goes:
time: 185 us
  waiting for transfers between devices  89.9 us (49%)
  matrix products  72.3 us (39%)
  between operations  13.5 us (7%)
  local copies, waits for them, and re-layouts  4.89 us (3%)
  starting transfers between devices  3.84 us (2%)
    dot_general x1, matrix products, body(): lax.dot_general(scaled, col_block, (((1,), (0,)), ((), ())), precision=la...  72.3 us
    all_gather x1, waiting for transfers between devices, body(): own_block = lax.all_gather(mel, 'row', axis=1, tiled=True)  56.1 us
    all_gather x1, waiting for transfers between devices, body(): rows_all = lax.all_gather(mel, 'col', axis=0, tiled=True)  16.4 us
    all_to_all x1, waiting for transfers between devices, body(): lax.all_to_all(own_block, 'col', split_axis=1, concat_axis=0, tiled=True)  16 us
    all_to_all x1, starting transfers between devices, body(): lax.all_to_all(own_block, 'col', split_axis=1, concat_axis=0, tiled=True)  3.8 us
  transfers between devices with their start and end apart: 3, of which 3 were waited for; matrix products, arithmetic and copies ran while one was open for 3% of the time, Pallas kernels for 0%

commit v1 on v0

--- a/solution.py
+++ b/solution.py
@@ -8,7 +8,12 @@
 
 
 def body(mel, pair_val, pair_cond, val_energy, cond_energy, freqs):
-    rows_all = lax.all_gather(mel, "col", axis=0, tiled=True)
+    ring = [mel]
+    for hop in range(3):
+        ring.append(lax.ppermute(ring[-1], "col", [(dev, (dev + 1) % 4) for dev in range(4)]))
+    rows_all = jnp.roll(
+        jnp.concatenate(ring[::-1], axis=0), (lax.axis_index("col") + 1) * ring[0].shape[0], axis=0
+    )
     own_block = lax.all_gather(mel, "row", axis=1, tiled=True)
     col_block = lax.all_to_all(own_block, "col", split_axis=1, concat_axis=0, tiled=True)
     cond_onehot = (

time: 185 us -> 179 us (0.968)
  waiting for transfers between devices: 89.9 us -> 73.9 us
  local copies, waits for them, and re-layouts: 4.89 us -> 13.1 us
    all_gather x1, waiting for transfers between devices: 56.1 us -> 35.2 us  [body(): own_block = lax.all_gather(mel, 'row', axis=1, tiled=True)]
    ppermute x0 -> x3, waiting for transfers between devices: none -> 17.2 us  [body(): lax.ppermute(ring[-1], 'col', [(dev, (dev + 1) % 4) for dev in range(4)])]
    all_gather x1 -> x0, waiting for transfers between devices: 16.4 us -> none  [body(): rows_all = lax.all_gather(mel, 'col', axis=0, tiled=True)]
    unnamed x10 -> x9, local copies, waits for them, and re-layouts: 0.02 us -> 5.15 us
    all_to_all x1, waiting for transfers between devices: 16 us -> 20.8 us  [body(): lax.all_to_all(own_block, 'col', split_axis=1, concat_axis=0, tiled=True)]
    dynamic_slice x0 -> x2, local copies, waits for them, and re-layouts: none -> 3.98 us  [body(): jnp.roll(jnp.concatenate(ring[::-1], axis=0), (lax.axis_index('col') + 1)...]
  transfers between devices with their start and end apart: 3 -> 5, of which waited for: 3 -> 5; matrix products, arithmetic and copies ran while one was open for 3% -> 6% of each run, Pallas kernels for 0% -> 0%
where the time goes in v1:
time: 179 us
  waiting for transfers between devices  73.9 us (41%)
  matrix products  72.3 us (40%)
  between operations  13.4 us (7%)
  local copies, waits for them, and re-layouts  13.1 us (7%)
  starting transfers between devices  4.35 us (2%)
    dot_general x1, matrix products, body(): lax.dot_general(scaled, col_block, (((1,), (0,)), ((), ())), precision=la...  72.3 us
    all_gather x1, waiting for transfers between devices, body(): own_block = lax.all_gather(mel, 'row', axis=1, tiled=True)  35.2 us
    all_to_all x1, waiting for transfers between devices, body(): lax.all_to_all(own_block, 'col', split_axis=1, concat_axis=0, tiled=True)  20.8 us
    ppermute x3, waiting for transfers between devices, body(): lax.ppermute(ring[-1], 'col', [(dev, (dev + 1) % 4) for dev in range(4)])  17.2 us
    unnamed x9, local copies, waits for them, and re-layouts  5.15 us
    dynamic_slice x2, local copies, waits for them, and re-layouts, body(): jnp.roll(jnp.concatenate(ring[::-1], axis=0), (lax.axis_index('col') + 1)...  3.98 us
    all_to_all x1, starting transfers between devices, body(): lax.all_to_all(own_block, 'col', split_axis=1, concat_axis=0, tiled=True)  3.76 us
  transfers between devices with their start and end apart: 5, of which 5 were waited for; matrix products, arithmetic and copies ran while one was open for 6% of the time, Pallas kernels for 0%

profile of v1, /device:TPU:0, one launch (start us, length us, event | category | flops | bytes accessed | tf_op | source)
XLA Modules:
  0.0 178.7 jit_solution(10945525864663286185)
XLA Ops:
  6.5 0.0 all-gather.2.cloned.1.call-start
  6.5 0.7 all-gather.2.cloned.1.call-update
  7.3 0.5 collective-permute-start
  7.8 6.6 %collective-permute-done = f32[32,2304]{1,0:T(8,128)S(1)} collective-permute-done((f32[32,2304]{1,0:T(8,128)}, f32[32,2304]{1,0:T(8,128)S(1)}, u32[]{:S(2)}, u32[]{:S(2)}) %collective-permute-start) | collective-permute-done | bytes 294944 | tf_op jit(solution)/shard_map/ppermute | solution.py:13
  14.4 0.0 collective-permute-start.1
  14.4 0.8 select_reduce_fusion
  15.2 5.3 %collective-permute-done.1 = f32[32,2304]{1,0:T(8,128)S(1)} collective-permute-done((f32[32,2304]{1,0:T(8,128)S(1)}, f32[32,2304]{1,0:T(8,128)S(1)}, u32[]{:S(2)}, u32[]{:S(2)}) %collective-permute-start.1) | collective-permute-done | bytes 294944 | tf_op jit(solution)/shard_map/ppermute | solution.py:13
  20.5 0.0 collective-permute-start.2
  20.5 0.7 mul.72
  21.3 0.1 divide_multiply_fusion
  21.3 5.3 %collective-permute-done.2 = f32[32,2304]{1,0:T(8,128)S(1)} collective-permute-done((f32[32,2304]{1,0:T(8,128)S(1)}, f32[32,2304]{1,0:T(8,128)S(1)}, u32[]{:S(2)}, u32[]{:S(2)}) %collective-permute-start.2) | collective-permute-done | bytes 294944 | tf_op jit(solution)/shard_map/ppermute | solution.py:13
  26.7 0.7 constant_dynamic-update-slice_fusion.7
  27.4 0.7 constant_dynamic-update-slice_fusion.6
  28.1 0.7 constant_dynamic-update-slice_fusion.5
  28.9 35.2 %all-gather.2.cloned.1.call-done = f32[32,18432]{1,0:T(8,128)} async-done(((f32[32,2304]{1,0:T(8,128)}), f32[32,18432]{1,0:T(8,128)}) %all-gather.2.cloned.1.call-update) | async-done | bytes 2359312 | tf_op jit(solution)/shard_map/all_gather | solution.py:17
  64.1 3.2 %copy.13 = f32[4,4,8,4608]{3,2,0,1:T(8,128)} copy(f32[4,4,8,4608]{3,2,1,0:T(8,128)} %bitcast.13) | data formatting | bytes 4718592 | tf_op jit(solution)/shard_map/all_to_all | solution.py:18
  67.3 0.0 copy-start
  67.3 3.8 %all-to-all-start = ((f32[32,4,4608]{2,0,1:T(8,128)}), f32[32,4,4608]{2,0,1:T(8,128)S(1)}, u32[]{:S(2)}, u32[]{:S(2)}) async-start(f32[32,4,4608]{2,0,1:T(8,128)} %bitcast.12), calls=%async_computation | async-start | bytes 4718592 | tf_op jit(solution)/shard_map/all_to_all | solution.py:18
  71.1 0.0 copy-done
  71.1 0.7 constant_dynamic-update-slice_fusion.4
  71.9 0.7 constant_dynamic-update-slice_fusion.3
  72.6 0.7 constant_dynamic-update-slice_fusion.2
  73.3 0.7 constant_dynamic-update-slice_fusion.1
  74.0 0.8 constant_dynamic-update-slice_fusion
  74.8 2.4 %constant_dynamic-slice_fusion = f32[128,2304]{1,0:T(8,128)} fusion(f32[256,2304]{1,0:T(8,128)} %constant_dynamic-update-slice_fusion, s32[]{:T(128)S(6)} %select_n.14), kind=kLoop, calls=%fused_computation.18 | loop fusion | bytes 2359300 | tf_op jit(solution)/shard_map/jit(_roll_dynamic)/dynamic_slice | solution.py:14
  77.1 1.6 copy.9
  78.8 20.8 %all-to-all-done = f32[32,4,4608]{2,0,1:T(8,128)S(1)} async-done(((f32[32,4,4608]{2,0,1:T(8,128)}), f32[32,4,4608]{2,0,1:T(8,128)S(1)}, u32[]{:S(2)}, u32[]{:S(2)}) %all-to-all-start) | async-done | bytes 2359328 | tf_op jit(solution)/shard_map/all_to_all | solution.py:18
  99.6 72.3 %fusion = f32[2,2304,4608]{2,1,0:T(8,128)} fusion(f32[128,4608,1]{1,0,2:T(8,128)S(1)} %bitcast.11, f32[128,2304]{0,1:T(8,128)S(1)} %copy.9, f32[2,128]{1,0:T(2,128)S(1)} %divide_multiply_fusion), kind=kOutput, calls=%fused_computation.1 | convolution fusion | flops 32615497728 | bytes 88474624 | tf_op jit(solution)/shard_map/dot_general | solution.py:36
  (1 shorter events, 0.0 us)
Async XLA Ops:
  6.5 57.6 %all-gather.2.cloned.1.call-start = ((), (), s32[]{:S(2)}) async-start(), calls=%async_computation.1 | async-start | bytes 2654208 | tf_op jit(solution)/shard_map/all_gather | solution.py:17
  7.3 7.1 %collective-permute-start = (f32[32,2304]{1,0:T(8,128)}, f32[32,2304]{1,0:T(8,128)S(1)}, u32[]{:S(2)}, u32[]{:S(2)}) collective-permute-start(f32[32,2304]{1,0:T(8,128)} %param.6), channel_id=1, source_target_pairs={{0,1},{1,2},{2,3},{3,0},{4,5},{5,6},{6,7},{7,4},{8,9},{9,10},{10,1... | collective-permute-start | bytes 884744 | tf_op jit(solution)/shard_map/ppermute | solution.py:13
  14.4 6.1 %collective-permute-start.1 = (f32[32,2304]{1,0:T(8,128)S(1)}, f32[32,2304]{1,0:T(8,128)S(1)}, u32[]{:S(2)}, u32[]{:S(2)}) collective-permute-start(f32[32,2304]{1,0:T(8,128)S(1)} %collective-permute-done), channel_id=1, source_target_pairs={{0,1},{1,2},{2,3},{3,0},{4,5},{5,6},{6,7},{7,4},{8,9},{9,10},{10,1... | collective-permute-start | bytes 884744 | tf_op jit(solution)/shard_map/ppermute | solution.py:13
  20.5 6.1 %collective-permute-start.2 = (f32[32,2304]{1,0:T(8,128)S(1)}, f32[32,2304]{1,0:T(8,128)S(1)}, u32[]{:S(2)}, u32[]{:S(2)}) collective-permute-start(f32[32,2304]{1,0:T(8,128)S(1)} %collective-permute-done.1), channel_id=1, source_target_pairs={{0,1},{1,2},{2,3},{3,0},{4,5},{5,6},{6,7},{7,4},{8,9},{9,10},{10,1... | collective-permute-start | bytes 884744 | tf_op jit(solution)/shard_map/ppermute | solution.py:13
  67.3 3.8 %copy-start = (f32[32,2304]{1,0:T(8,128)S(1)}, f32[32,2304]{1,0:T(8,128)}, u32[]{:S(2)}) copy-start(f32[32,2304]{1,0:T(8,128)} %param.6) | copy-start | bytes 884740
  67.3 32.2 %all-to-all-start = ((f32[32,4,4608]{2,0,1:T(8,128)}), f32[32,4,4608]{2,0,1:T(8,128)S(1)}, u32[]{:S(2)}, u32[]{:S(2)}) async-start(f32[32,4,4608]{2,0,1:T(8,128)} %bitcast.12), calls=%async_computation | async-start | bytes 4718592 | tf_op jit(solution)/shard_map/all_to_all | solution.py:18
Sparse Core Ops, SparseCore 0:
  9.5 54.5 all-gather.1
